TPU v7x, 32 devices: a whole 2x2x4 slice. The times are simulated.
32 devices in a mesh: lon: 8 (over y, x, core), lat: 4 (over z).
Axes of the slice: x: 2, y: 2, z: 4, core: 2. Of those that a mesh axis runs over, the one named last changes fastest.
Arguments:
- latent: bfloat16 [4, 64, 128, 320], P(None, 'lat', 'lon'), may hold values from -28 to 28, as said below
- norm1_gain: float32 [320], replicated, may hold values from 0.1 to 1.9
- norm1_shift: float32 [320], replicated, may hold values from -3 to 3
- conv1_weight: bfloat16 [3, 3, 320, 320], replicated, may hold values from -0.109375 to 0.109375
- conv1_bias: float32 [320], replicated, may hold values from -3 to 3
- emb_shift: float32 [4, 320], replicated, may hold values from -4 to 4
- norm2_gain: float32 [320], replicated, may hold values from 0.1 to 1.9
- norm2_shift: float32 [320], replicated, may hold values from -3 to 3
- conv2_weight: bfloat16 [3, 3, 320, 320], replicated, may hold values from -0.109375 to 0.109375
- conv2_bias: float32 [320], replicated, may hold values from -3 to 3
Outputs:
- block_out: bfloat16 [4, 64, 128, 320], P(None, 'lat', 'lon')
Inputs may be any that keep to these rules, and one draw needn't show every extreme that they name: `latent`: Real-valued activations.
All inputs are finite; a program needn't handle non-finite values.
Results may differ from a plain program's by a relative error of at most 0.007.
Values may be sent and summed in bfloat16 or wider, within the bound.
No kernel may reach another device: no remote copies, remote signals or barrier semaphores. Data moves between devices by JAX's collectives and lax.ppermute only.
A program may use at most 64 MiB of HBM per device.

v0:
```python
import jax
import jax.numpy as jnp
from jax import lax
from jax.sharding import PartitionSpec as P

GROUPS = 32


def padded_2(array, sides, width, wrap):
    for axis, dim in sides:
        devices, length = (lax.axis_size(axis), array.shape[dim])
        up = [(i, (i + 1) % devices) for i in range(devices if wrap else devices - 1)]
        down = [(j, i) for i, j in up]
        last = lax.slice_in_dim(array, length - width, length, axis=dim)
        leading = lax.slice_in_dim(array, 0, width, axis=dim)
        before = lax.ppermute(last, axis, up)
        after = lax.ppermute(leading, axis, down)
        array = jnp.concatenate([before, array, after], axis=dim)
    return array


def from_behind(array, axis, by):
    devices = lax.axis_size(axis)
    return lax.ppermute(array, axis, [(i, (i + by) % devices) for i in range(devices)])


def group_stats(field, cell_count):
    frame_count = field.shape[0]
    grouped = field.reshape(frame_count, -1, GROUPS, field.shape[3] // GROUPS)
    summed, squares = lax.psum(
        (jnp.sum(grouped, axis=(1, 3)), jnp.sum(grouped * grouped, axis=(1, 3))), ("lon", "lat")
    )
    average = summed / cell_count
    variance = squares / cell_count - average * average
    return (average, lax.rsqrt(variance + 1e-05))


def activate(field, average, inverse, norm_gain, norm_shift):
    per_group = field.shape[3] // GROUPS
    per_mean = jnp.repeat(average, per_group, axis=1)[:, None, None, :]
    per_inverse = jnp.repeat(inverse, per_group, axis=1)[:, None, None, :]
    normed = (field - per_mean) * per_inverse * norm_gain + norm_shift
    return jax.nn.silu(normed).astype(jnp.bfloat16)


def sphere_pad(field):
    side_padded = padded_2(field, (("lon", 2),), 1, True)
    both_padded = padded_2(side_padded, (("lat", 1),), 1, False)
    north_row, south_row = from_behind(
        (side_padded[:, 0], side_padded[:, -1]), "lon", lax.axis_size("lon") // 2
    )
    lat_index = lax.axis_index("lat")
    first_row = jnp.where(lat_index == 0, north_row, both_padded[:, 0])
    final_row = jnp.where(lat_index == lax.axis_size("lat") - 1, south_row, both_padded[:, -1])
    return jnp.concatenate([first_row[:, None], both_padded[:, 1:-1], final_row[:, None]], axis=1)


def padded_input(source, cell_count, norm_gain, norm_shift):
    source_f = source.astype(jnp.float32)
    average, inverse = group_stats(source_f, cell_count)
    return sphere_pad(activate(source_f, average, inverse, norm_gain, norm_shift))


def convolve(padded, weight):
    return lax.conv_general_dilated(
        padded,
        weight,
        (1, 1),
        "VALID",
        dimension_numbers=("NHWC", "HWIO", "NHWC"),
        preferred_element_type=jnp.float32,
    )


def on_device(
    latent,
    norm1_gain,
    norm1_shift,
    conv1_weight,
    conv1_bias,
    emb_shift,
    norm2_gain,
    norm2_shift,
    conv2_weight,
    conv2_bias,
):
    per_group = latent.shape[3] // GROUPS
    cell_count = (
        latent.shape[1] * latent.shape[2] * lax.axis_size("lat") * lax.axis_size("lon") * per_group
    )
    first_padded = padded_input(latent, cell_count, norm1_gain, norm1_shift)
    hidden = convolve(first_padded, conv1_weight) + conv1_bias + emb_shift[:, None, None, :]
    hidden = hidden.astype(jnp.bfloat16)
    second_padded = padded_input(hidden, cell_count, norm2_gain, norm2_shift)
    branch = convolve(second_padded, conv2_weight) + conv2_bias
    return (latent.astype(jnp.float32) + branch).astype(jnp.bfloat16)


def solution(mesh):
    placed = (P(None, "lat", "lon", None), P(), P(), P(), P(), P(), P(), P(), P(), P())
    return jax.shard_map(
        on_device,
        mesh=mesh,
        in_specs=placed,
        out_specs=P(None, "lat", "lon", None),
        check_vma=False,
    )
```

profile of v0, /device:TPU:0, one launch (start us, length us, event | category | flops | bytes accessed | tf_op | source)
XLA Modules:
  0.0 154.9 jit_solution(12832509377845679093)
XLA Ops:
  0.0 2.1 %convert_reduce_fusion = (f32[4,320]{1,0:T(4,128)S(1)}, f32[4,320]{1,0:T(4,128)S(1)}) fusion(bf16[4,16,16,320]{3,2,1,0:T(8,128)(2,1)} %param.10), kind=kLoop, calls=%fused_computation.6 | loop fusion | flops 1308160 | bytes 665600 | tf_op jit(solution)/shard_map/reduce_sum | solution.py:31
  2.1 0.1 reduce_sum.47
  2.2 0.1 reduce_sum.53
  2.4 0.1 reduce_sum.51
  2.5 0.1 reduce_sum.54
  2.6 42.0 %all-reduce.1 = (f32[4,32]{1,0:T(4,128)S(1)}, f32[4,32]{1,0:T(4,128)S(1)}) all-reduce(f32[4,32]{1,0:T(4,128)S(1)} %reduce_sum.54, f32[4,32]{1,0:T(4,128)S(1)} %reduce_sum.51), channel_id=1, replica_groups=mesh['lon'=8,'lat'=4] {'lon','lat'}, use_global_device_ids=true, to_apply=%region_5.6 | all-reduce | flops 256 | bytes 2048 | tf_op jit(solution)/shard_map/psum | solution.py:30
  44.6 0.1 sub.26
  44.8 0.1 mul.59
  45.0 2.4 %fusion.18 = bf16[4,16,16,320]{3,0,2,1:T(4,128)(2,1)S(1)} fusion(f32[320]{0:T(512)} %param.12, f32[320]{0:T(512)} %param.11, f32[4,320]{1,0:T(4,128)S(1)} %mul.59, f32[4,320]{1,0:T(4,128)S(1)} %sub.26, bf16[4,16,16,320]{3,2,1,0:T(8,128)(2,1)} %param.10), kind=kLoop, calls=%fused_computation.32 | loop fusion | flops 3276800 | bytes 1323520 | tf_op jit(solution)/shard_map/convert_element_type | solution.py:43
  47.5 2.6 %collective-permute-start.1 = (bf16[4,16,1,320]{3,0,2,1:T(4,128)(2,1)S(1)}, bf16[4,16,1,320]{3,0,2,1:T(4,128)(2,1)S(1)}, u32[]{:S(2)}, u32[]{:S(2)}) collective-permute-start(bf16[4,16,1,320]{3,0,2,1:T(4,128)(2,1)S(1)} %get-tuple-element.18), channel_id=1, source_target_pairs={{4,0},{8,4},{12,8},{16,12},{20,16},{24,20},{28,24},{0,28},{5,1},{9... | collective-permute-start | bytes 122888 | tf_op jit(solution)/shard_map/ppermute | solution.py:17
  50.1 1.8 %collective-permute-done = bf16[4,16,1,320]{3,0,2,1:T(4,128)(2,1)S(1)} collective-permute-done((bf16[4,16,1,320]{3,0,2,1:T(4,128)(2,1)S(1)}, bf16[4,16,1,320]{3,0,2,1:T(4,128)(2,1)S(1)}, u32[]{:S(2)}, u32[]{:S(2)}) %collective-permute-start) | collective-permute-done | bytes 40992 | tf_op jit(solution)/shard_map/ppermute | solution.py:16
  51.9 0.1 pad_maximum_fusion.5
  52.0 2.3 %collective-permute-start.4 = (bf16[4,18,320]{2,0,1:T(4,128)(2,1)S(1)}, bf16[4,18,320]{2,0,1:T(4,128)(2,1)S(1)}, u32[]{:S(2)}, u32[]{:S(2)}) collective-permute-start(bf16[4,18,320]{2,0,1:T(4,128)(2,1)S(1)} %bitcast.78), channel_id=1, source_target_pairs={{0,16},{4,20},{8,24},{12,28},{16,0},{20,4},{24,8},{28,12},{1,17},{... | collective-permute-start | bytes 138248 | tf_op jit(solution)/shard_map/ppermute | solution.py:24
  54.3 1.3 collective-permute-start.5
  55.6 4.7 %collective-permute-start.3 = (bf16[4,1,18,320]{3,0,2,1:T(4,128)(2,1)S(1)}, bf16[4,1,18,320]{3,0,2,1:T(4,128)(2,1)S(1)}, u32[]{:S(2)}, u32[]{:S(2)}) collective-permute-start(bf16[4,1,18,320]{3,0,2,1:T(4,128)(2,1)S(1)} %get-tuple-element.14), channel_id=1, source_target_pairs={{0,1},{1,2},{2,3},{4,5},{5,6},{6,7},{8,9},{9,10},{10,11},{12,13},{... | collective-permute-start | bytes 138248 | tf_op jit(solution)/shard_map/ppermute | solution.py:16
  60.4 0.1 collective-permute-start.2
  60.5 4.1 %collective-permute-done.2 = bf16[4,18,320]{2,0,1:T(4,128)(2,1)S(1)} collective-permute-done((bf16[4,18,320]{2,0,1:T(4,128)(2,1)S(1)}, bf16[4,18,320]{2,0,1:T(4,128)(2,1)S(1)}, u32[]{:S(2)}, u32[]{:S(2)}) %collective-permute-start.2) | collective-permute-done | bytes 46112 | tf_op jit(solution)/shard_map/ppermute | solution.py:24
  64.6 0.9 maximum_bitcast_fusion.1
  65.6 0.5 pad
  66.1 0.3 slice.44
  66.4 1.0 fusion.5
  67.5 0.2 broadcast.25
  67.6 0.5 copy-done.7
  68.1 7.1 %fusion.30 = (f32[16,32,3,320]{3,1,2,0:T(8,128)S(1)}, f32[16,32,3,320]{3,1,2,0:T(8,128)}) fusion(f32[16,32,3,320]{3,0,2,1:T(8,128)S(1)} %bitcast.75, f32[320]{0:T(512)S(1)} %copy-done.7, bf16[3,3,320,320]{3,2,1,0:T(8,128)(2,1)S(1)} %copy-done, bf16[18,4,8,5,320]{4,1,3,2,0:T(4,128)(2,1)S(1)} %fusion.5, pred[32,3]{0,1:T(4,128)(4,1)S(1)} %copy-done.9), kind=kOutput, calls=%fused_computation.59 | convolution fusion | flops 2834104320 | bytes 9586016 | tf_op jit(solution)/shard_map/conv_general_dilated | solution.py:65
  75.2 1.4 copy.121
  76.6 0.1 slice_reduce_fusion
  76.7 0.1 reduce_sum.74
  76.8 0.1 reduce_sum.75
  76.9 3.0 %copy.119 = f32[16,32,3,320]{3,0,2,1:T(8,128)S(1)} copy(f32[16,32,3,320]{3,1,2,0:T(8,128)} %get-tuple-element.24) | data formatting | bytes 3932160 | tf_op jit(solution)/shard_map/convert_element_type | solution.py:59
  79.9 0.1 slice_reduce_fusion.1
  80.0 0.1 reduce_sum.59
  80.2 0.1 reduce_sum.72
  80.2 39.4 %all-reduce = (f32[4,32]{1,0:T(4,128)S(1)}, f32[4,32]{1,0:T(4,128)S(1)}) all-reduce(f32[4,32]{1,0:T(4,128)S(1)} %reduce_sum.75, f32[4,32]{1,0:T(4,128)S(1)} %reduce_sum.72), channel_id=1, replica_groups=mesh['lon'=8,'lat'=4] {'lon','lat'}, use_global_device_ids=true, to_apply=%region_11.12 | all-reduce | flops 256 | bytes 2048 | tf_op jit(solution)/shard_map/psum | solution.py:30
  119.7 0.1 sub.30
  119.9 0.1 mul.67
  120.1 0.2 broadcast.27
  120.3 0.2 broadcast.26
  120.4 1.3 copy-done.1
  121.7 1.8 %multiply_convert_fusion = bf16[16,32,3,320]{3,1,2,0:T(8,128)(2,1)S(1)} fusion(f32[16,32,3,320]{3,0,2,1:T(8,128)S(1)} %bitcast.65, f32[16,32,3,320]{3,1,2,0:T(8,128)S(1)} %copy-done.1, f32[16,32,3,320]{3,0,2,1:T(8,128)S(1)} %bitcast.66, f32[320]{0:T(512)S(1)} %copy-done.4, f32[320]{0:T(512)S(1)} %copy-done.5), kind=kLoop, calls=%fused_computation.14 | loop fusion | flops 4423680 | bytes 6883840 | tf_op jit(solution)/shard_map/convert_element_type | solution.py:43
  123.5 0.4 copy.123
  123.9 0.1 slice_bitcast_fusion
  124.1 2.6 %collective-permute-start.7 = (bf16[4,16,1,320]{3,1,2,0:T(8,128)(2,1)S(1)}, bf16[4,16,1,320]{3,1,2,0:T(8,128)(2,1)S(1)}, u32[]{:S(2)}, u32[]{:S(2)}) collective-permute-start(bf16[4,16,1,320]{3,1,2,0:T(8,128)(2,1)S(1)} %get-tuple-element.16), channel_id=1, source_target_pairs={{4,0},{8,4},{12,8},{16,12},{20,16},{24,20},{28,24},{0,28},{5,1},{9... | collective-permute-start | bytes 122888 | tf_op jit(solution)/shard_map/ppermute | solution.py:17
  126.7 1.8 %collective-permute-done.6 = bf16[4,16,1,320]{3,1,2,0:T(8,128)(2,1)S(1)} collective-permute-done((bf16[4,16,1,320]{3,1,2,0:T(8,128)(2,1)S(1)}, bf16[4,16,1,320]{3,1,2,0:T(8,128)(2,1)S(1)}, u32[]{:S(2)}, u32[]{:S(2)}) %collective-permute-start.6) | collective-permute-done | bytes 40992 | tf_op jit(solution)/shard_map/ppermute | solution.py:16
  128.5 0.2 pad_maximum_fusion.2
  128.7 2.3 %collective-permute-start.10 = (bf16[4,18,320]{2,0,1:T(4,128)(2,1)S(1)}, bf16[4,18,320]{2,0,1:T(4,128)(2,1)S(1)}, u32[]{:S(2)}, u32[]{:S(2)}) collective-permute-start(bf16[4,18,320]{2,0,1:T(4,128)(2,1)S(1)} %bitcast.77), channel_id=1, source_target_pairs={{0,16},{4,20},{8,24},{12,28},{16,0},{20,4},{24,8},{28,12},{1,17},{... | collective-permute-start | bytes 138248 | tf_op jit(solution)/shard_map/ppermute | solution.py:24
  131.1 1.3 collective-permute-start.11
  132.4 4.6 %collective-permute-start.9 = (bf16[4,1,18,320]{3,1,2,0:T(2,128)(2,1)S(1)}, bf16[4,1,18,320]{3,1,2,0:T(2,128)(2,1)S(1)}, u32[]{:S(2)}, u32[]{:S(2)}) collective-permute-start(bf16[4,1,18,320]{3,1,2,0:T(2,128)(2,1)S(1)} %get-tuple-element.12), channel_id=1, source_target_pairs={{0,1},{1,2},{2,3},{4,5},{5,6},{6,7},{8,9},{9,10},{10,11},{12,13},{... | collective-permute-start | bytes 138248 | tf_op jit(solution)/shard_map/ppermute | solution.py:16
  137.0 0.1 collective-permute-start.8
  137.1 0.6 collective-permute-done.11
  137.8 0.1 copy.129
  137.9 3.3 %collective-permute-done.8 = bf16[4,18,320]{2,0,1:T(4,128)(2,1)S(1)} collective-permute-done((bf16[4,18,320]{2,0,1:T(4,128)(2,1)S(1)}, bf16[4,18,320]{2,0,1:T(4,128)(2,1)S(1)}, u32[]{:S(2)}, u32[]{:S(2)}) %collective-permute-start.8) | collective-permute-done | bytes 46112 | tf_op jit(solution)/shard_map/ppermute | solution.py:24
  141.2 0.1 copy.128
  141.3 0.9 maximum_bitcast_fusion
  142.2 0.4 copy.136
  142.6 0.5 pad.2.clone
  143.1 0.3 slice.50
  143.4 1.0 fusion.6
  144.5 0.5 copy-done.6
  145.0 5.0 %select_add_fusion = f32[16,32,3,320]{3,1,2,0:T(8,128)S(1)} fusion(bf16[3,3,320,320]{3,2,1,0:T(8,128)(2,1)S(1)} %copy-done.6, bf16[18,4,8,5,320]{4,1,3,2,0:T(4,128)(2,1)S(1)} %fusion.6, f32[320]{0:T(512)S(1)} %copy-done.8, pred[32,3]{0,1:T(4,128)(4,1)S(1)} %copy-done.9), kind=kOutput, calls=%fused_computation.13 | convolution fusion | flops 2832138240 | bytes 5653856 | tf_op jit(solution)/shard_map/conv_general_dilated | solution.py:65
  150.0 1.4 copy.132
  151.4 0.1 slice.51
  151.5 1.0 copy-done.2
  152.5 1.4 fusion.17
  154.0 1.0 copy.134
  (39 shorter events, 0.8 us)
Async XLA Ops:
  0.0 67.6 %copy-start = (bf16[3,3,320,320]{3,2,1,0:T(8,128)(2,1)S(1)}, bf16[3,3,320,320]{3,2,1,0:T(8,128)(2,1)}, u32[]{:S(2)}) copy-start(bf16[3,3,320,320]{3,2,1,0:T(8,128)(2,1)} %param.13) | copy-start | bytes 5529604
  47.4 4.5 %collective-permute-start = (bf16[4,16,1,320]{3,0,2,1:T(4,128)(2,1)S(1)}, bf16[4,16,1,320]{3,0,2,1:T(4,128)(2,1)S(1)}, u32[]{:S(2)}, u32[]{:S(2)}) collective-permute-start(bf16[4,16,1,320]{3,0,2,1:T(4,128)(2,1)S(1)} %get-tuple-element.17), channel_id=1, source_target_pairs={{0,4},{4,8},{8,12},{12,16},{16,20},{20,24},{24,28},{28,0},{1,5},{5... | collective-permute-start | bytes 122888 | tf_op jit(solution)/shard_map/ppermute | solution.py:16
  47.5 4.4 %collective-permute-start.1 = (bf16[4,16,1,320]{3,0,2,1:T(4,128)(2,1)S(1)}, bf16[4,16,1,320]{3,0,2,1:T(4,128)(2,1)S(1)}, u32[]{:S(2)}, u32[]{:S(2)}) collective-permute-start(bf16[4,16,1,320]{3,0,2,1:T(4,128)(2,1)S(1)} %get-tuple-element.18), channel_id=1, source_target_pairs={{4,0},{8,4},{12,8},{16,12},{20,16},{24,20},{28,24},{0,28},{5,1},{9... | collective-permute-start | bytes 122888 | tf_op jit(solution)/shard_map/ppermute | solution.py:17
  52.0 8.5 %collective-permute-start.4 = (bf16[4,18,320]{2,0,1:T(4,128)(2,1)S(1)}, bf16[4,18,320]{2,0,1:T(4,128)(2,1)S(1)}, u32[]{:S(2)}, u32[]{:S(2)}) collective-permute-start(bf16[4,18,320]{2,0,1:T(4,128)(2,1)S(1)} %bitcast.78), channel_id=1, source_target_pairs={{0,16},{4,20},{8,24},{12,28},{16,0},{20,4},{24,8},{28,12},{1,17},{... | collective-permute-start | bytes 138248 | tf_op jit(solution)/shard_map/ppermute | solution.py:24
  54.3 6.1 %collective-permute-start.5 = (bf16[4,1,18,320]{3,0,2,1:T(4,128)(2,1)S(1)}, bf16[4,1,18,320]{3,0,2,1:T(4,128)(2,1)S(1)}, u32[]{:S(2)}, u32[]{:S(2)}) collective-permute-start(bf16[4,1,18,320]{3,0,2,1:T(4,128)(2,1)S(1)} %get-tuple-element.13), channel_id=1, source_target_pairs={{1,0},{2,1},{3,2},{5,4},{6,5},{7,6},{9,8},{10,9},{11,10},{13,12},{... | collective-permute-start | bytes 138248 | tf_op jit(solution)/shard_map/ppermute | solution.py:17
  55.6 9.0 %collective-permute-start.3 = (bf16[4,1,18,320]{3,0,2,1:T(4,128)(2,1)S(1)}, bf16[4,1,18,320]{3,0,2,1:T(4,128)(2,1)S(1)}, u32[]{:S(2)}, u32[]{:S(2)}) collective-permute-start(bf16[4,1,18,320]{3,0,2,1:T(4,128)(2,1)S(1)} %get-tuple-element.14), channel_id=1, source_target_pairs={{0,1},{1,2},{2,3},{4,5},{5,6},{6,7},{8,9},{9,10},{10,11},{12,13},{... | collective-permute-start | bytes 138248 | tf_op jit(solution)/shard_map/ppermute | solution.py:16
  60.4 4.2 %collective-permute-start.2 = (bf16[4,18,320]{2,0,1:T(4,128)(2,1)S(1)}, bf16[4,18,320]{2,0,1:T(4,128)(2,1)S(1)}, u32[]{:S(2)}, u32[]{:S(2)}) collective-permute-start(bf16[4,18,320]{2,0,1:T(4,128)(2,1)S(1)} %bitcast.79), channel_id=1, source_target_pairs={{0,16},{4,20},{8,24},{12,28},{16,0},{20,4},{24,8},{28,12},{1,17},{... | collective-permute-start | bytes 138248 | tf_op jit(solution)/shard_map/ppermute | solution.py:24
  66.4 1.1 copy-start.3
  67.4 0.7 copy-start.7
  67.4 0.7 copy-start.9
  120.1 1.7 %copy-start.1 = (f32[16,32,3,320]{3,1,2,0:T(8,128)S(1)}, f32[16,32,3,320]{3,1,2,0:T(8,128)}, u32[]{:S(2)}) copy-start(f32[16,32,3,320]{3,1,2,0:T(8,128)} %get-tuple-element.24) | copy-start | bytes 5898244
  120.1 1.7 %copy-start.4 = (f32[320]{0:T(512)S(1)}, f32[320]{0:T(512)}, u32[]{:S(2)}) copy-start(f32[320]{0:T(512)} %param.17) | copy-start | bytes 3844
  120.1 1.7 %copy-start.5 = (f32[320]{0:T(512)S(1)}, f32[320]{0:T(512)}, u32[]{:S(2)}) copy-start(f32[320]{0:T(512)} %param.16) | copy-start | bytes 3844
  124.0 4.5 %collective-permute-start.6 = (bf16[4,16,1,320]{3,1,2,0:T(8,128)(2,1)S(1)}, bf16[4,16,1,320]{3,1,2,0:T(8,128)(2,1)S(1)}, u32[]{:S(2)}, u32[]{:S(2)}) collective-permute-start(bf16[4,16,1,320]{3,1,2,0:T(8,128)(2,1)S(1)} %get-tuple-element.15), channel_id=1, source_target_pairs={{0,4},{4,8},{8,12},{12,16},{16,20},{20,24},{24,28},{28,0},{1,5},{5... | collective-permute-start | bytes 122888 | tf_op jit(solution)/shard_map/ppermute | solution.py:16
  124.1 4.4 %collective-permute-start.7 = (bf16[4,16,1,320]{3,1,2,0:T(8,128)(2,1)S(1)}, bf16[4,16,1,320]{3,1,2,0:T(8,128)(2,1)S(1)}, u32[]{:S(2)}, u32[]{:S(2)}) collective-permute-start(bf16[4,16,1,320]{3,1,2,0:T(8,128)(2,1)S(1)} %get-tuple-element.16), channel_id=1, source_target_pairs={{4,0},{8,4},{12,8},{16,12},{20,16},{24,20},{28,24},{0,28},{5,1},{9... | collective-permute-start | bytes 122888 | tf_op jit(solution)/shard_map/ppermute | solution.py:17
  128.7 8.3 %collective-permute-start.10 = (bf16[4,18,320]{2,0,1:T(4,128)(2,1)S(1)}, bf16[4,18,320]{2,0,1:T(4,128)(2,1)S(1)}, u32[]{:S(2)}, u32[]{:S(2)}) collective-permute-start(bf16[4,18,320]{2,0,1:T(4,128)(2,1)S(1)} %bitcast.77), channel_id=1, source_target_pairs={{0,16},{4,20},{8,24},{12,28},{16,0},{20,4},{24,8},{28,12},{1,17},{... | collective-permute-start | bytes 138248 | tf_op jit(solution)/shard_map/ppermute | solution.py:24
  131.1 6.6 %collective-permute-start.11 = (bf16[4,1,18,320]{3,1,2,0:T(2,128)(2,1)S(1)}, bf16[4,1,18,320]{3,1,2,0:T(2,128)(2,1)S(1)}, u32[]{:S(2)}, u32[]{:S(2)}) collective-permute-start(bf16[4,1,18,320]{3,1,2,0:T(2,128)(2,1)S(1)} %get-tuple-element.11), channel_id=1, source_target_pairs={{1,0},{2,1},{3,2},{5,4},{6,5},{7,6},{9,8},{10,9},{11,10},{13,12},{... | collective-permute-start | bytes 138248 | tf_op jit(solution)/shard_map/ppermute | solution.py:17
  132.4 8.8 %collective-permute-start.9 = (bf16[4,1,18,320]{3,1,2,0:T(2,128)(2,1)S(1)}, bf16[4,1,18,320]{3,1,2,0:T(2,128)(2,1)S(1)}, u32[]{:S(2)}, u32[]{:S(2)}) collective-permute-start(bf16[4,1,18,320]{3,1,2,0:T(2,128)(2,1)S(1)} %get-tuple-element.12), channel_id=1, source_target_pairs={{0,1},{1,2},{2,3},{4,5},{5,6},{6,7},{8,9},{9,10},{10,11},{12,13},{... | collective-permute-start | bytes 138248 | tf_op jit(solution)/shard_map/ppermute | solution.py:16
  137.0 4.2 %collective-permute-start.8 = (bf16[4,18,320]{2,0,1:T(4,128)(2,1)S(1)}, bf16[4,18,320]{2,0,1:T(4,128)(2,1)S(1)}, u32[]{:S(2)}, u32[]{:S(2)}) collective-permute-start(bf16[4,18,320]{2,0,1:T(4,128)(2,1)S(1)} %bitcast.76), channel_id=1, source_target_pairs={{0,16},{4,20},{8,24},{12,28},{16,0},{20,4},{24,8},{28,12},{1,17},{... | collective-permute-start | bytes 138248 | tf_op jit(solution)/shard_map/ppermute | solution.py:24
  143.4 1.6 %copy-start.6 = (bf16[3,3,320,320]{3,2,1,0:T(8,128)(2,1)S(1)}, bf16[3,3,320,320]{3,2,1,0:T(8,128)(2,1)}, u32[]{:S(2)}) copy-start(bf16[3,3,320,320]{3,2,1,0:T(8,128)(2,1)} %param.18) | copy-start | bytes 5529604
  143.4 1.6 %copy-start.8 = (f32[320]{0:T(512)S(1)}, f32[320]{0:T(512)}, u32[]{:S(2)}) copy-start(f32[320]{0:T(512)} %param.19) | copy-start | bytes 3844
  151.4 1.1 copy-start.2
where the time goes:
time: 156 us; the launch traced here: 155 us
  blocking collectives  81.4 us (52%)
  starting transfers between devices  22.1 us (14%)
  local copies, waits for them, and re-layouts  14.6 us (9%)
  other arithmetic  12.7 us (8%)
  matrix products  12.1 us (8%)
  waiting for transfers between devices  11.6 us (7%)
    psum x2, blocking collectives, group_stats(): lax.psum((jnp.sum(grouped, axis=(1, 3)), jnp.sum(grouped * grouped, axis=...  81.4 us
    conv_general_dilated x2, matrix products, convolve(): lax.conv_general_dilated(padded, weight, (1, 1), 'VALID', dimension_numbe...  12.1 us
    ppermute x4, starting transfers between devices, padded_2(): before = lax.ppermute(last, axis, up)  9.4 us
    ppermute x4, starting transfers between devices, padded_2(): after = lax.ppermute(leading, axis, down)  7.82 us
    ppermute x4, waiting for transfers between devices, from_behind(): lax.ppermute(array, axis, [(i, (i + by) % devices) for i in range(devices)])  7.42 us
    ppermute x4, starting transfers between devices, from_behind(): lax.ppermute(array, axis, [(i, (i + by) % devices) for i in range(devices)])  4.85 us
    convert_element_type x2, other arithmetic, activate(): return jax.nn.silu(normed).astype(jnp.bfloat16)  4.24 us
    unnamed x21, local copies, waits for them, and re-layouts  3.76 us
  transfers between devices with their start and end apart: 12, of which 5 were waited for; matrix products, arithmetic and copies ran while one was open for 0% of the time, Pallas kernels for 0%

commit v1 on v0

--- a/solution.py
+++ b/solution.py
@@ -28,7 +28,8 @@
     frame_count = field.shape[0]
     grouped = field.reshape(frame_count, -1, GROUPS, field.shape[3] // GROUPS)
     summed, squares = lax.psum(
-        (jnp.sum(grouped, axis=(1, 3)), jnp.sum(grouped * grouped, axis=(1, 3))), ("lon", "lat")
+        lax.psum((jnp.sum(grouped, axis=(1, 3)), jnp.sum(grouped * grouped, axis=(1, 3))), "lat"),
+        "lon",
     )
     average = summed / cell_count
     variance = squares / cell_count - average * average

time: 156 us -> 118 us (0.76)
  blocking collectives: 81.4 us -> 45.7 us
    psum x2, blocking collectives: 81.4 us -> 21.9 us  [group_stats(): lax.psum((jnp.sum(grouped, axis=(1, 3)), jnp.sum(grouped * grouped, axis=...]
    psum x0 -> x2, blocking collectives: none -> 23.8 us  [group_stats(): lax.psum(lax.psum((jnp.sum(grouped, axis=(1, 3)), jnp.sum(grouped * group...]
  transfers between devices with their start and end apart: 12 -> 12, of which waited for: 5 -> 4; matrix products, arithmetic and copies ran while one was open for 0% -> 0% of each run, Pallas kernels for 0% -> 0%
where the time goes in v1:
time: 118 us; the launch traced here: 117 us
  blocking collectives  45.7 us (39%)
  starting transfers between devices  21.5 us (18%)
  local copies, waits for them, and re-layouts  14.6 us (12%)
  other arithmetic  12.7 us (11%)
  matrix products  12.1 us (10%)
  waiting for transfers between devices  10.4 us (9%)
    psum x2, blocking collectives, group_stats(): lax.psum(lax.psum((jnp.sum(grouped, axis=(1, 3)), jnp.sum(grouped * group...  23.8 us
    psum x2, blocking collectives, group_stats(): lax.psum((jnp.sum(grouped, axis=(1, 3)), jnp.sum(grouped * grouped, axis=...  21.9 us
    conv_general_dilated x2, matrix products, convolve(): lax.conv_general_dilated(padded, weight, (1, 1), 'VALID', dimension_numbe...  12.1 us
    ppermute x4, starting transfers between devices, padded_2(): before = lax.ppermute(last, axis, up)  9.4 us
    ppermute x4, starting transfers between devices, padded_2(): after = lax.ppermute(leading, axis, down)  7.82 us
    ppermute x4, waiting for transfers between devices, from_behind(): lax.ppermute(array, axis, [(i, (i + by) % devices) for i in range(devices)])  6.36 us
    ppermute x4, starting transfers between devices, from_behind(): lax.ppermute(array, axis, [(i, (i + by) % devices) for i in range(devices)])  4.31 us
    convert_element_type x2, other arithmetic, activate(): return jax.nn.silu(normed).astype(jnp.bfloat16)  4.24 us
  transfers between devices with their start and end apart: 12, of which 4 were waited for; matrix products, arithmetic and copies ran while one was open for 0% of the time, Pallas kernels for 0%

profile of v1, /device:TPU:0, one launch (start us, length us, event | category | flops | bytes accessed | tf_op | source)
XLA Modules:
  0.0 117.4 jit_solution(14688770237298395738)
XLA Ops:
  0.0 2.1 %convert_reduce_fusion = (f32[4,320]{1,0:T(4,128)S(1)}, f32[4,320]{1,0:T(4,128)S(1)}) fusion(bf16[4,16,16,320]{3,2,1,0:T(8,128)(2,1)} %param.10), kind=kLoop, calls=%fused_computation.6 | loop fusion | flops 1308160 | bytes 665600 | tf_op jit(solution)/shard_map/reduce_sum | solution.py:31
  2.1 0.1 reduce_sum.47
  2.2 0.1 reduce_sum.53
  2.4 0.1 reduce_sum.51
  2.5 0.1 reduce_sum.54
  2.6 13.5 %all-reduce.3 = (f32[4,32]{1,0:T(4,128)S(1)}, f32[4,32]{1,0:T(4,128)S(1)}) all-reduce(f32[4,32]{1,0:T(4,128)S(1)} %reduce_sum.54, f32[4,32]{1,0:T(4,128)S(1)} %reduce_sum.51), channel_id=1, replica_groups=mesh['lon'=8,'lat'=4] {'lat'}, use_global_device_ids=true, to_apply=%region_6.7 | all-reduce | flops 256 | bytes 2048 | tf_op jit(solution)/shard_map/psum | solution.py:31
  16.0 11.8 %all-reduce.1 = (f32[4,32]{1,0:T(4,128)S(1)}, f32[4,32]{1,0:T(4,128)S(1)}) all-reduce(f32[4,32]{1,0:T(4,128)S(1)} %get-tuple-element.13, f32[4,32]{1,0:T(4,128)S(1)} %get-tuple-element.14), channel_id=1, replica_groups=mesh['lon'=8,'lat'=4] {'lon'}, use_global_device_ids=true, to_apply=%region_7.8 | all-reduce | flops 256 | bytes 2048 | tf_op jit(solution)/shard_map/psum | solution.py:30
  27.9 0.1 sub.26
  28.1 0.1 mul.59
  28.3 2.4 %fusion.18 = bf16[4,16,16,320]{3,0,2,1:T(4,128)(2,1)S(1)} fusion(f32[320]{0:T(512)} %param.12, f32[320]{0:T(512)} %param.11, f32[4,320]{1,0:T(4,128)S(1)} %mul.59, f32[4,320]{1,0:T(4,128)S(1)} %sub.26, bf16[4,16,16,320]{3,2,1,0:T(8,128)(2,1)} %param.10), kind=kLoop, calls=%fused_computation.32 | loop fusion | flops 3276800 | bytes 1323520 | tf_op jit(solution)/shard_map/convert_element_type | solution.py:44
  30.8 2.6 %collective-permute-start.1 = (bf16[4,16,1,320]{3,0,2,1:T(4,128)(2,1)S(1)}, bf16[4,16,1,320]{3,0,2,1:T(4,128)(2,1)S(1)}, u32[]{:S(2)}, u32[]{:S(2)}) collective-permute-start(bf16[4,16,1,320]{3,0,2,1:T(4,128)(2,1)S(1)} %get-tuple-element.22), channel_id=1, source_target_pairs={{4,0},{8,4},{12,8},{16,12},{20,16},{24,20},{28,24},{0,28},{5,1},{9... | collective-permute-start | bytes 122888 | tf_op jit(solution)/shard_map/ppermute | solution.py:17
  33.5 2.2 %collective-permute-done = bf16[4,16,1,320]{3,0,2,1:T(4,128)(2,1)S(1)} collective-permute-done((bf16[4,16,1,320]{3,0,2,1:T(4,128)(2,1)S(1)}, bf16[4,16,1,320]{3,0,2,1:T(4,128)(2,1)S(1)}, u32[]{:S(2)}, u32[]{:S(2)}) %collective-permute-start) | collective-permute-done | bytes 40992 | tf_op jit(solution)/shard_map/ppermute | solution.py:16
  35.6 0.1 pad_maximum_fusion.5
  35.7 1.2 %collective-permute-start.4 = (bf16[4,18,320]{2,0,1:T(4,128)(2,1)S(1)}, bf16[4,18,320]{2,0,1:T(4,128)(2,1)S(1)}, u32[]{:S(2)}, u32[]{:S(2)}) collective-permute-start(bf16[4,18,320]{2,0,1:T(4,128)(2,1)S(1)} %bitcast.78), channel_id=1, source_target_pairs={{0,16},{4,20},{8,24},{12,28},{16,0},{20,4},{24,8},{28,12},{1,17},{... | collective-permute-start | bytes 138248 | tf_op jit(solution)/shard_map/ppermute | solution.py:24
  36.9 1.3 %collective-permute-start.5 = (bf16[4,1,18,320]{3,0,2,1:T(4,128)(2,1)S(1)}, bf16[4,1,18,320]{3,0,2,1:T(4,128)(2,1)S(1)}, u32[]{:S(2)}, u32[]{:S(2)}) collective-permute-start(bf16[4,1,18,320]{3,0,2,1:T(4,128)(2,1)S(1)} %get-tuple-element.17), channel_id=1, source_target_pairs={{1,0},{2,1},{3,2},{5,4},{6,5},{7,6},{9,8},{10,9},{11,10},{13,12},{... | collective-permute-start | bytes 138248 | tf_op jit(solution)/shard_map/ppermute | solution.py:17
  38.2 4.7 %collective-permute-start.3 = (bf16[4,1,18,320]{3,0,2,1:T(4,128)(2,1)S(1)}, bf16[4,1,18,320]{3,0,2,1:T(4,128)(2,1)S(1)}, u32[]{:S(2)}, u32[]{:S(2)}) collective-permute-start(bf16[4,1,18,320]{3,0,2,1:T(4,128)(2,1)S(1)} %get-tuple-element.18), channel_id=1, source_target_pairs={{0,1},{1,2},{2,3},{4,5},{5,6},{6,7},{8,9},{9,10},{10,11},{12,13},{... | collective-permute-start | bytes 138248 | tf_op jit(solution)/shard_map/ppermute | solution.py:16
  43.0 0.9 collective-permute-start.2
  43.9 3.2 %collective-permute-done.2 = bf16[4,18,320]{2,0,1:T(4,128)(2,1)S(1)} collective-permute-done((bf16[4,18,320]{2,0,1:T(4,128)(2,1)S(1)}, bf16[4,18,320]{2,0,1:T(4,128)(2,1)S(1)}, u32[]{:S(2)}, u32[]{:S(2)}) %collective-permute-start.2) | collective-permute-done | bytes 46112 | tf_op jit(solution)/shard_map/ppermute | solution.py:24
  47.2 0.9 maximum_bitcast_fusion.1
  48.1 0.5 pad
  48.6 0.3 slice.44
  48.9 1.0 fusion.5
  50.0 0.2 broadcast.25
  50.2 0.5 copy-done.7
  50.7 7.1 %fusion.30 = (f32[16,32,3,320]{3,1,2,0:T(8,128)S(1)}, f32[16,32,3,320]{3,1,2,0:T(8,128)}) fusion(f32[16,32,3,320]{3,0,2,1:T(8,128)S(1)} %bitcast.75, f32[320]{0:T(512)S(1)} %copy-done.7, bf16[3,3,320,320]{3,2,1,0:T(8,128)(2,1)S(1)} %copy-done, bf16[18,4,8,5,320]{4,1,3,2,0:T(4,128)(2,1)S(1)} %fusion.5, pred[32,3]{0,1:T(4,128)(4,1)S(1)} %copy-done.9), kind=kOutput, calls=%fused_computation.59 | convolution fusion | flops 2834104320 | bytes 9586016 | tf_op jit(solution)/shard_map/conv_general_dilated | solution.py:66
  57.7 1.4 %copy.121 = f32[16,32,3,320]{3,0,2,1:T(8,128)S(1)} copy(f32[16,32,3,320]{3,1,2,0:T(8,128)S(1)} %get-tuple-element.27) | data formatting | bytes 3932160 | tf_op jit(solution)/shard_map/mul | solution.py:31
  59.1 0.1 slice_reduce_fusion
  59.2 0.1 reduce_sum.74
  59.3 0.1 reduce_sum.75
  59.4 3.0 %copy.119 = f32[16,32,3,320]{3,0,2,1:T(8,128)S(1)} copy(f32[16,32,3,320]{3,1,2,0:T(8,128)} %get-tuple-element.28) | data formatting | bytes 3932160 | tf_op jit(solution)/shard_map/convert_element_type | solution.py:60
  62.5 0.1 slice_reduce_fusion.1
  62.6 0.1 reduce_sum.59
  62.7 0.1 reduce_sum.72
  62.8 8.4 %all-reduce.2 = (f32[4,32]{1,0:T(4,128)S(1)}, f32[4,32]{1,0:T(4,128)S(1)}) all-reduce(f32[4,32]{1,0:T(4,128)S(1)} %reduce_sum.75, f32[4,32]{1,0:T(4,128)S(1)} %reduce_sum.72), channel_id=1, replica_groups=mesh['lon'=8,'lat'=4] {'lat'}, use_global_device_ids=true, to_apply=%region_14.15 | all-reduce | flops 256 | bytes 2048 | tf_op jit(solution)/shard_map/psum | solution.py:31
  71.2 12.0 %all-reduce = (f32[4,32]{1,0:T(4,128)S(1)}, f32[4,32]{1,0:T(4,128)S(1)}) all-reduce(f32[4,32]{1,0:T(4,128)S(1)} %get-tuple-element.11, f32[4,32]{1,0:T(4,128)S(1)} %get-tuple-element.12), channel_id=1, replica_groups=mesh['lon'=8,'lat'=4] {'lon'}, use_global_device_ids=true, to_apply=%region_15.16 | all-reduce | flops 256 | bytes 2048 | tf_op jit(solution)/shard_map/psum | solution.py:30
  83.3 0.1 sub.30
  83.5 0.1 mul.67
  83.6 0.2 broadcast.27
  83.8 0.2 broadcast.26
  84.0 1.3 %copy-done.1 = f32[16,32,3,320]{3,1,2,0:T(8,128)S(1)} copy-done((f32[16,32,3,320]{3,1,2,0:T(8,128)S(1)}, f32[16,32,3,320]{3,1,2,0:T(8,128)}, u32[]{:S(2)}) %copy-start.1) | copy-done | bytes 1966104
  85.3 1.8 %multiply_convert_fusion = bf16[16,32,3,320]{3,1,2,0:T(8,128)(2,1)S(1)} fusion(f32[16,32,3,320]{3,0,2,1:T(8,128)S(1)} %bitcast.65, f32[16,32,3,320]{3,1,2,0:T(8,128)S(1)} %copy-done.1, f32[16,32,3,320]{3,0,2,1:T(8,128)S(1)} %bitcast.66, f32[320]{0:T(512)S(1)} %copy-done.4, f32[320]{0:T(512)S(1)} %copy-done.5), kind=kLoop, calls=%fused_computation.14 | loop fusion | flops 4423680 | bytes 6883840 | tf_op jit(solution)/shard_map/convert_element_type | solution.py:44
  87.1 0.4 copy.123
  87.6 2.6 %collective-permute-start.7 = (bf16[4,16,1,320]{3,1,2,0:T(8,128)(2,1)S(1)}, bf16[4,16,1,320]{3,1,2,0:T(8,128)(2,1)S(1)}, u32[]{:S(2)}, u32[]{:S(2)}) collective-permute-start(bf16[4,16,1,320]{3,1,2,0:T(8,128)(2,1)S(1)} %get-tuple-element.20), channel_id=1, source_target_pairs={{4,0},{8,4},{12,8},{16,12},{20,16},{24,20},{28,24},{0,28},{5,1},{9... | collective-permute-start | bytes 122888 | tf_op jit(solution)/shard_map/ppermute | solution.py:17
  90.3 1.8 %collective-permute-done.6 = bf16[4,16,1,320]{3,1,2,0:T(8,128)(2,1)S(1)} collective-permute-done((bf16[4,16,1,320]{3,1,2,0:T(8,128)(2,1)S(1)}, bf16[4,16,1,320]{3,1,2,0:T(8,128)(2,1)S(1)}, u32[]{:S(2)}, u32[]{:S(2)}) %collective-permute-start.6) | collective-permute-done | bytes 40992 | tf_op jit(solution)/shard_map/ppermute | solution.py:16
  92.1 0.2 pad_maximum_fusion.2
  92.3 1.2 %collective-permute-start.10 = (bf16[4,18,320]{2,0,1:T(4,128)(2,1)S(1)}, bf16[4,18,320]{2,0,1:T(4,128)(2,1)S(1)}, u32[]{:S(2)}, u32[]{:S(2)}) collective-permute-start(bf16[4,18,320]{2,0,1:T(4,128)(2,1)S(1)} %bitcast.77), channel_id=1, source_target_pairs={{0,16},{4,20},{8,24},{12,28},{16,0},{20,4},{24,8},{28,12},{1,17},{... | collective-permute-start | bytes 138248 | tf_op jit(solution)/shard_map/ppermute | solution.py:24
  93.6 1.3 %collective-permute-start.11 = (bf16[4,1,18,320]{3,1,2,0:T(2,128)(2,1)S(1)}, bf16[4,1,18,320]{3,1,2,0:T(2,128)(2,1)S(1)}, u32[]{:S(2)}, u32[]{:S(2)}) collective-permute-start(bf16[4,1,18,320]{3,1,2,0:T(2,128)(2,1)S(1)} %get-tuple-element.15), channel_id=1, source_target_pairs={{1,0},{2,1},{3,2},{5,4},{6,5},{7,6},{9,8},{10,9},{11,10},{13,12},{... | collective-permute-start | bytes 138248 | tf_op jit(solution)/shard_map/ppermute | solution.py:17
  94.9 4.6 %collective-permute-start.9 = (bf16[4,1,18,320]{3,1,2,0:T(2,128)(2,1)S(1)}, bf16[4,1,18,320]{3,1,2,0:T(2,128)(2,1)S(1)}, u32[]{:S(2)}, u32[]{:S(2)}) collective-permute-start(bf16[4,1,18,320]{3,1,2,0:T(2,128)(2,1)S(1)} %get-tuple-element.16), channel_id=1, source_target_pairs={{0,1},{1,2},{2,3},{4,5},{5,6},{6,7},{8,9},{9,10},{10,11},{12,13},{... | collective-permute-start | bytes 138248 | tf_op jit(solution)/shard_map/ppermute | solution.py:16
  99.4 0.9 collective-permute-start.8
  100.4 0.1 copy.129
  100.5 3.1 %collective-permute-done.8 = bf16[4,18,320]{2,0,1:T(4,128)(2,1)S(1)} collective-permute-done((bf16[4,18,320]{2,0,1:T(4,128)(2,1)S(1)}, bf16[4,18,320]{2,0,1:T(4,128)(2,1)S(1)}, u32[]{:S(2)}, u32[]{:S(2)}) %collective-permute-start.8) | collective-permute-done | bytes 46112 | tf_op jit(solution)/shard_map/ppermute | solution.py:24
  103.7 0.1 copy.128
  103.8 0.9 maximum_bitcast_fusion
  104.7 0.4 copy.136
  105.1 0.5 pad.2.clone
  105.6 0.3 slice.50
  105.9 1.0 fusion.6
  106.9 0.5 copy-done.6
  107.5 5.0 %select_add_fusion = f32[16,32,3,320]{3,1,2,0:T(8,128)S(1)} fusion(bf16[3,3,320,320]{3,2,1,0:T(8,128)(2,1)S(1)} %copy-done.6, bf16[18,4,8,5,320]{4,1,3,2,0:T(4,128)(2,1)S(1)} %fusion.6, f32[320]{0:T(512)S(1)} %copy-done.8, pred[32,3]{0,1:T(4,128)(4,1)S(1)} %copy-done.9), kind=kOutput, calls=%fused_computation.13 | convolution fusion | flops 2832138240 | bytes 5653856 | tf_op jit(solution)/shard_map/conv_general_dilated | solution.py:66
  112.5 1.4 %copy.132 = f32[16,32,3,320]{3,0,2,1:T(8,128)S(1)} copy(f32[16,32,3,320]{3,1,2,0:T(8,128)S(1)} %select_add_fusion) | data formatting | bytes 3932160 | tf_op jit(solution)/shard_map/add | solution.py:96
  113.9 0.1 slice.51
  114.0 1.0 copy-done.2
  115.0 1.4 %fusion.17 = bf16[4,16,16,320]{3,0,2,1:T(4,128)(2,1)S(1)} fusion(f32[16,4,16,320]{3,0,2,1:T(8,128)S(1)} %slice.51, bf16[4,16,16,320]{3,2,1,0:T(8,128)(2,1)S(1)} %copy-done.2), kind=kLoop, calls=%fused_computation.28 | loop fusion | flops 983040 | bytes 2621440 | tf_op jit(solution)/shard_map/convert_element_type | solution.py:97
  116.4 1.0 copy.134
  (41 shorter events, 0.8 us)
Async XLA Ops:
  0.0 50.2 %copy-start = (bf16[3,3,320,320]{3,2,1,0:T(8,128)(2,1)S(1)}, bf16[3,3,320,320]{3,2,1,0:T(8,128)(2,1)}, u32[]{:S(2)}) copy-start(bf16[3,3,320,320]{3,2,1,0:T(8,128)(2,1)} %param.13) | copy-start | bytes 5529604
  30.8 4.9 %collective-permute-start = (bf16[4,16,1,320]{3,0,2,1:T(4,128)(2,1)S(1)}, bf16[4,16,1,320]{3,0,2,1:T(4,128)(2,1)S(1)}, u32[]{:S(2)}, u32[]{:S(2)}) collective-permute-start(bf16[4,16,1,320]{3,0,2,1:T(4,128)(2,1)S(1)} %get-tuple-element.21), channel_id=1, source_target_pairs={{0,4},{4,8},{8,12},{12,16},{16,20},{20,24},{24,28},{28,0},{1,5},{5... | collective-permute-start | bytes 122888 | tf_op jit(solution)/shard_map/ppermute | solution.py:16
  30.8 4.8 %collective-permute-start.1 = (bf16[4,16,1,320]{3,0,2,1:T(4,128)(2,1)S(1)}, bf16[4,16,1,320]{3,0,2,1:T(4,128)(2,1)S(1)}, u32[]{:S(2)}, u32[]{:S(2)}) collective-permute-start(bf16[4,16,1,320]{3,0,2,1:T(4,128)(2,1)S(1)} %get-tuple-element.22), channel_id=1, source_target_pairs={{4,0},{8,4},{12,8},{16,12},{20,16},{24,20},{28,24},{0,28},{5,1},{9... | collective-permute-start | bytes 122888 | tf_op jit(solution)/shard_map/ppermute | solution.py:17
  35.7 8.2 %collective-permute-start.4 = (bf16[4,18,320]{2,0,1:T(4,128)(2,1)S(1)}, bf16[4,18,320]{2,0,1:T(4,128)(2,1)S(1)}, u32[]{:S(2)}, u32[]{:S(2)}) collective-permute-start(bf16[4,18,320]{2,0,1:T(4,128)(2,1)S(1)} %bitcast.78), channel_id=1, source_target_pairs={{0,16},{4,20},{8,24},{12,28},{16,0},{20,4},{24,8},{28,12},{1,17},{... | collective-permute-start | bytes 138248 | tf_op jit(solution)/shard_map/ppermute | solution.py:24
  36.9 7.0 %collective-permute-start.5 = (bf16[4,1,18,320]{3,0,2,1:T(4,128)(2,1)S(1)}, bf16[4,1,18,320]{3,0,2,1:T(4,128)(2,1)S(1)}, u32[]{:S(2)}, u32[]{:S(2)}) collective-permute-start(bf16[4,1,18,320]{3,0,2,1:T(4,128)(2,1)S(1)} %get-tuple-element.17), channel_id=1, source_target_pairs={{1,0},{2,1},{3,2},{5,4},{6,5},{7,6},{9,8},{10,9},{11,10},{13,12},{... | collective-permute-start | bytes 138248 | tf_op jit(solution)/shard_map/ppermute | solution.py:17
  38.2 9.0 %collective-permute-start.3 = (bf16[4,1,18,320]{3,0,2,1:T(4,128)(2,1)S(1)}, bf16[4,1,18,320]{3,0,2,1:T(4,128)(2,1)S(1)}, u32[]{:S(2)}, u32[]{:S(2)}) collective-permute-start(bf16[4,1,18,320]{3,0,2,1:T(4,128)(2,1)S(1)} %get-tuple-element.18), channel_id=1, source_target_pairs={{0,1},{1,2},{2,3},{4,5},{5,6},{6,7},{8,9},{9,10},{10,11},{12,13},{... | collective-permute-start | bytes 138248 | tf_op jit(solution)/shard_map/ppermute | solution.py:16
  43.0 4.2 %collective-permute-start.2 = (bf16[4,18,320]{2,0,1:T(4,128)(2,1)S(1)}, bf16[4,18,320]{2,0,1:T(4,128)(2,1)S(1)}, u32[]{:S(2)}, u32[]{:S(2)}) collective-permute-start(bf16[4,18,320]{2,0,1:T(4,128)(2,1)S(1)} %bitcast.79), channel_id=1, source_target_pairs={{0,16},{4,20},{8,24},{12,28},{16,0},{20,4},{24,8},{28,12},{1,17},{... | collective-permute-start | bytes 138248 | tf_op jit(solution)/shard_map/ppermute | solution.py:24
  48.9 1.1 copy-start.3
  50.0 0.7 copy-start.7
  50.0 0.7 copy-start.9
  83.6 1.7 %copy-start.1 = (f32[16,32,3,320]{3,1,2,0:T(8,128)S(1)}, f32[16,32,3,320]{3,1,2,0:T(8,128)}, u32[]{:S(2)}) copy-start(f32[16,32,3,320]{3,1,2,0:T(8,128)} %get-tuple-element.28) | copy-start | bytes 5898244
  83.6 1.7 %copy-start.4 = (f32[320]{0:T(512)S(1)}, f32[320]{0:T(512)}, u32[]{:S(2)}) copy-start(f32[320]{0:T(512)} %param.17) | copy-start | bytes 3844
  83.6 1.7 %copy-start.5 = (f32[320]{0:T(512)S(1)}, f32[320]{0:T(512)}, u32[]{:S(2)}) copy-start(f32[320]{0:T(512)} %param.16) | copy-start | bytes 3844
  87.6 4.5 %collective-permute-start.6 = (bf16[4,16,1,320]{3,1,2,0:T(8,128)(2,1)S(1)}, bf16[4,16,1,320]{3,1,2,0:T(8,128)(2,1)S(1)}, u32[]{:S(2)}, u32[]{:S(2)}) collective-permute-start(bf16[4,16,1,320]{3,1,2,0:T(8,128)(2,1)S(1)} %get-tuple-element.19), channel_id=1, source_target_pairs={{0,4},{4,8},{8,12},{12,16},{16,20},{20,24},{24,28},{28,0},{1,5},{5... | collective-permute-start | bytes 122888 | tf_op jit(solution)/shard_map/ppermute | solution.py:16
  87.6 4.5 %collective-permute-start.7 = (bf16[4,16,1,320]{3,1,2,0:T(8,128)(2,1)S(1)}, bf16[4,16,1,320]{3,1,2,0:T(8,128)(2,1)S(1)}, u32[]{:S(2)}, u32[]{:S(2)}) collective-permute-start(bf16[4,16,1,320]{3,1,2,0:T(8,128)(2,1)S(1)} %get-tuple-element.20), channel_id=1, source_target_pairs={{4,0},{8,4},{12,8},{16,12},{20,16},{24,20},{28,24},{0,28},{5,1},{9... | collective-permute-start | bytes 122888 | tf_op jit(solution)/shard_map/ppermute | solution.py:17
  92.3 8.0 %collective-permute-start.10 = (bf16[4,18,320]{2,0,1:T(4,128)(2,1)S(1)}, bf16[4,18,320]{2,0,1:T(4,128)(2,1)S(1)}, u32[]{:S(2)}, u32[]{:S(2)}) collective-permute-start(bf16[4,18,320]{2,0,1:T(4,128)(2,1)S(1)} %bitcast.77), channel_id=1, source_target_pairs={{0,16},{4,20},{8,24},{12,28},{16,0},{20,4},{24,8},{28,12},{1,17},{... | collective-permute-start | bytes 138248 | tf_op jit(solution)/shard_map/ppermute | solution.py:24
  93.6 6.8 %collective-permute-start.11 = (bf16[4,1,18,320]{3,1,2,0:T(2,128)(2,1)S(1)}, bf16[4,1,18,320]{3,1,2,0:T(2,128)(2,1)S(1)}, u32[]{:S(2)}, u32[]{:S(2)}) collective-permute-start(bf16[4,1,18,320]{3,1,2,0:T(2,128)(2,1)S(1)} %get-tuple-element.15), channel_id=1, source_target_pairs={{1,0},{2,1},{3,2},{5,4},{6,5},{7,6},{9,8},{10,9},{11,10},{13,12},{... | collective-permute-start | bytes 138248 | tf_op jit(solution)/shard_map/ppermute | solution.py:17
  94.9 8.8 %collective-permute-start.9 = (bf16[4,1,18,320]{3,1,2,0:T(2,128)(2,1)S(1)}, bf16[4,1,18,320]{3,1,2,0:T(2,128)(2,1)S(1)}, u32[]{:S(2)}, u32[]{:S(2)}) collective-permute-start(bf16[4,1,18,320]{3,1,2,0:T(2,128)(2,1)S(1)} %get-tuple-element.16), channel_id=1, source_target_pairs={{0,1},{1,2},{2,3},{4,5},{5,6},{6,7},{8,9},{9,10},{10,11},{12,13},{... | collective-permute-start | bytes 138248 | tf_op jit(solution)/shard_map/ppermute | solution.py:16
  99.4 4.2 %collective-permute-start.8 = (bf16[4,18,320]{2,0,1:T(4,128)(2,1)S(1)}, bf16[4,18,320]{2,0,1:T(4,128)(2,1)S(1)}, u32[]{:S(2)}, u32[]{:S(2)}) collective-permute-start(bf16[4,18,320]{2,0,1:T(4,128)(2,1)S(1)} %bitcast.76), channel_id=1, source_target_pairs={{0,16},{4,20},{8,24},{12,28},{16,0},{20,4},{24,8},{28,12},{1,17},{... | collective-permute-start | bytes 138248 | tf_op jit(solution)/shard_map/ppermute | solution.py:24
  105.9 1.6 %copy-start.6 = (bf16[3,3,320,320]{3,2,1,0:T(8,128)(2,1)S(1)}, bf16[3,3,320,320]{3,2,1,0:T(8,128)(2,1)}, u32[]{:S(2)}) copy-start(bf16[3,3,320,320]{3,2,1,0:T(8,128)(2,1)} %param.18) | copy-start | bytes 5529604
  105.9 1.6 %copy-start.8 = (f32[320]{0:T(512)S(1)}, f32[320]{0:T(512)}, u32[]{:S(2)}) copy-start(f32[320]{0:T(512)} %param.19) | copy-start | bytes 3844
  113.9 1.1 copy-start.2
